TPU v7x, 32 devices: a whole 2x2x4 slice. The times are simulated.
32 devices in a mesh: samp: 8 (over y, x, core), sx: 2 (over z_hi), sy: 2 (over z_lo).
Axes of the slice: x: 2, y: 2, z: 4 (z_hi: 2, z_lo: 2; z = z_hi * 2 + z_lo), core: 2. Of those that a mesh axis runs over, the one named last changes fastest.
Arguments:
- volume: bfloat16 [8, 32, 4, 16, 128], P('samp', None, 'sx', 'sy'), may hold values from -6 to 6
- kernel: bfloat16 [64, 32, 3, 3, 3], replicated, may hold values from -0.21875 to 0.21875
- bias: float32 [64], replicated, may hold values from -4 to 4
- upstream: bfloat16 [8, 64, 4, 16, 128], P('samp', None, 'sx', 'sy'), may hold values from -6 to 6
Outputs:
- activated: bfloat16 [8, 64, 4, 16, 128], P('samp', None, 'sx', 'sy')
- input_grad: bfloat16 [8, 32, 4, 16, 128], P('samp', None, 'sx', 'sy')
- filter_grad: float32 [64, 32, 3, 3, 3], replicated
- bias_grad: float32 [64], replicated
All inputs are finite; a program needn't handle non-finite values.
Results may differ from a plain program's by a relative error of at most 0.0065.
Values may be sent and summed in bfloat16 or wider, within the bound.
A program may use at most 64 MiB of HBM per device.

v0:
```python
import jax
import jax.numpy as jnp
from jax import lax
from jax.sharding import PartitionSpec as P


def extended(shard, sides, width):
    for axis, dim in sides:
        size, length = (lax.axis_size(axis), shard.shape[dim])
        up = [(i, (i + 1) % size) for i in range(size - 1)]
        down = [(j, i) for i, j in up]
        last = lax.slice_in_dim(shard, length - width, length, axis=dim)
        initial = lax.slice_in_dim(shard, 0, width, axis=dim)
        before = lax.ppermute(last, axis, up)
        after = lax.ppermute(initial, axis, down)
        shard = jnp.concatenate([before, shard, after], axis=dim)
    return shard


def conv_forward(padded, kernel):
    return lax.conv_general_dilated(
        padded,
        kernel,
        (1, 1, 1),
        ((0, 0), (0, 0), (1, 1)),
        dimension_numbers=("NCDHW", "OIDHW", "NCDHW"),
        preferred_element_type=jnp.float32,
    )


def conv_backward(padded, kernel):
    flipped = kernel[:, :, ::-1, ::-1, ::-1]
    return lax.conv_general_dilated(
        padded,
        flipped,
        (1, 1, 1),
        ((0, 0), (0, 0), (1, 1)),
        dimension_numbers=("NCDHW", "IODHW", "NCDHW"),
        preferred_element_type=jnp.float32,
    )


def filter_terms(padded, delta):
    return lax.conv_general_dilated(
        padded,
        delta,
        (1, 1, 1),
        ((0, 0), (0, 0), (1, 1)),
        dimension_numbers=("CNDHW", "IODHW", "CNDHW"),
        preferred_element_type=jnp.float32,
    )


def slope_of(pre):
    return 0.3 + 0.7 * jax.nn.sigmoid(pre)


def per_device(volume, kernel, bias, upstream):
    samples, rows, cols, depth = (
        volume.shape[0],
        volume.shape[2],
        volume.shape[3],
        volume.shape[4],
    )
    bias_wide = bias[None, :, None, None, None]
    padded = extended(volume, (("sx", 2), ("sy", 3)), 1)
    pre = conv_forward(padded, kernel) + bias_wide
    delta = (upstream.astype(jnp.float32) * slope_of(pre)).astype(jnp.bfloat16)
    delta_pad = extended(delta, (("sx", 2), ("sy", 3)), 1)
    activated = (0.3 * pre + 0.7 * jax.nn.softplus(pre)).astype(jnp.bfloat16)
    input_grad = conv_backward(delta_pad, kernel).astype(jnp.bfloat16)
    wgrad = filter_terms(padded, delta)
    bgrad = jnp.sum(delta.astype(jnp.float32), axis=(0, 2, 3, 4))
    groups = lax.axis_size("sx") * lax.axis_size("sy")
    whole = lax.axis_size("samp") * samples * groups * rows * cols * depth
    norm = 1.0 / jnp.sqrt(jnp.float32(whole))
    wsum, bsum = lax.psum((wgrad, bgrad), ("samp", "sx", "sy"))
    return (activated, input_grad, wsum * norm, bsum * norm)


def solution(mesh):
    in_specs = (P("samp", None, "sx", "sy", None), P(), P(), P("samp", None, "sx", "sy", None))
    out_specs = (P("samp", None, "sx", "sy", None), P("samp", None, "sx", "sy", None), P(), P())
    return jax.shard_map(
        per_device, mesh=mesh, in_specs=in_specs, out_specs=out_specs, check_vma=False
    )
```

profile of v0, /device:TPU:8, one launch (start us, length us, event | category | flops | bytes accessed | tf_op | source)
XLA Modules:
  0.0 222.5 jit_solution(1578653945424406039)
XLA Ops:
  7.2 0.0 copy-start
  7.2 0.0 all-reduce.2.cloned.1.call-start
  7.2 0.9 fusion.47
  8.2 1.3 collective-permute-start.1
  9.5 5.4 %collective-permute-start = (bf16[1,32,1,8,128]{4,3,2,1,0:T(8,128)(2,1)S(1)}, bf16[1,32,1,8,128]{4,3,2,1,0:T(8,128)(2,1)S(1)}, u32[]{:S(2)}, u32[]{:S(2)}) collective-permute-start(bf16[1,32,1,8,128]{4,3,2,1,0:T(8,128)(2,1)S(1)} %get-tuple-element.26), channel_id=1, source_target_pairs={{0,2},{1,3},{4,6},{5,7},{8,10},{9,11},{12,14},{13,15},{16,18},{17,... | collective-permute-start | bytes 196616 | tf_op jit(solution)/shard_map/ppermute | solution.py:14
  14.9 0.3 collective-permute-done.1
  15.2 1.6 collective-permute-done
  16.8 1.0 pad_maximum_fusion.2
  17.8 0.0 copy-start.3
  17.8 1.2 copy.49
  19.0 1.3 fusion.44
  20.3 1.4 collective-permute-start.3
  21.7 1.3 collective-permute-start.2
  23.0 0.0 copy-done.3
  23.0 0.4 copy.57
  23.4 3.7 %collective-permute-done.3 = bf16[1,32,4,1,128]{1,0,4,3,2:T(2,128)(2,1)S(1)} collective-permute-done((bf16[1,32,4,1,128]{1,0,4,3,2:T(2,128)(2,1)}, bf16[1,32,4,1,128]{1,0,4,3,2:T(2,128)(2,1)S(1)}, u32[]{:S(2)}, u32[]{:S(2)}) %collective-permute-start.3) | collective-permute-done | bytes 32800 | tf_op jit(solution)/shard_map/ppermute | solution.py:15
  27.2 4.1 %collective-permute-done.2 = bf16[1,32,4,1,128]{1,0,4,3,2:T(2,128)(2,1)} collective-permute-done((bf16[1,32,4,1,128]{1,0,4,3,2:T(2,128)(2,1)}, bf16[1,32,4,1,128]{1,0,4,3,2:T(2,128)(2,1)}, u32[]{:S(2)}, u32[]{:S(2)}) %collective-permute-start.2) | collective-permute-done | bytes 32800 | tf_op jit(solution)/shard_map/ppermute | solution.py:14
  31.3 6.7 %pad_maximum_fusion = bf16[1,32,4,10,128]{1,0,4,3,2:T(2,128)(2,1)} fusion(bf16[1,32,4,1,128]{1,0,4,3,2:T(2,128)(2,1)S(1)} %collective-permute-done.3, bf16[1,32,4,8,128]{1,0,4,3,2:T(2,128)(2,1)S(1)} %copy.49, bf16[1,32,4,1,128]{1,0,4,3,2:T(2,128)(2,1)} %collective-permute-done.2), kind=kLoop, calls=%fused_computation.5 | loop fusion | flops 327680 | bytes 655360 | tf_op jit(solution)/shard_map/concatenate | solution.py:16
  38.1 4.7 %copy.52 = bf16[1,32,4,10,128]{4,1,3,2,0:T(8,128)(2,1)S(1)} copy(bf16[1,32,4,10,128]{1,0,4,3,2:T(2,128)(2,1)} %pad_maximum_fusion) | data formatting | bytes 655360 | tf_op jit(solution)/shard_map/concatenate | solution.py:16
  42.8 1.0 copy.69
  43.7 0.7 pad.clone
  44.4 0.0 copy-start.7
  44.4 0.0 copy-start.8
  44.5 0.2 copy.55
  44.7 0.0 copy-done
  44.7 0.4 copy-done.7
  45.1 0.0 copy-done.8
  45.1 3.4 %multiply_add_fusion = (f32[2,8,8,17,64]{4,2,3,1,0:T(8,128)S(1)}, bf16[2,8,8,17,64]{4,2,3,1,0:T(8,128)(2,1)}) fusion(f32[64]{0:T(128)S(1)} %copy-done.7, bf16[64,32,3,3,3]{0,1,4,3,2:T(8,128)(2,1)S(1)} %copy-done, bf16[32,4,10,1,7,2]{0,4,5,2,1,3:T(8,128)(2,1)S(1)} %slice.39, bf16[32,4,10,1,8,17]{0,4,5,2,1,3:T(8,128)(2,1)S(1)} %copy.55, ...), kind=kOutput, calls=%fused_computation.25 | convolution fusion | flops 244183040 | bytes 1330568 | tf_op jit(solution)/shard_map/conv_general_dilated | solution.py:21
  48.6 0.2 copy.58
  48.8 0.8 convert_reduce_fusion
  49.6 0.8 fusion.46
  50.4 0.1 copy-done.1
  50.5 15.8 %fusion.33 = f32[64,32,3,3,3]{0,1,4,3,2:T(8,128)} fusion(bf16[1,32,4,10,128]{1,0,4,3,2:T(2,128)(2,1)S(1)} %copy-done.1, bf16[1,64,2,8,128]{1,3,4,2,0:T(8,128)(2,1)S(1)} %get-tuple-element.17), kind=kOutput, calls=%fused_computation.31 | convolution fusion | flops 225312768 | bytes 811008 | tf_op jit(solution)/shard_map/conv_general_dilated | solution.py:44
  66.3 0.1 copy.56
  66.4 0.0 copy-start.6
  66.5 1.1 copy.67
  67.6 1.3 collective-permute-start.5
  68.9 0.0 copy-done.4
  68.9 5.5 %collective-permute-start.4 = (bf16[1,64,1,8,128]{1,3,4,2,0:T(8,128)(2,1)S(1)}, bf16[1,64,1,8,128]{1,3,4,2,0:T(8,128)(2,1)S(1)}, u32[]{:S(2)}, u32[]{:S(2)}) collective-permute-start(bf16[1,64,1,8,128]{1,3,4,2,0:T(8,128)(2,1)S(1)} %copy-done.4), channel_id=1, source_target_pairs={{0,2},{1,3},{4,6},{5,7},{8,10},{9,11},{12,14},{13,15},{16,18},{17,... | collective-permute-start | bytes 393224 | tf_op jit(solution)/shard_map/ppermute | solution.py:14
  74.4 0.0 all-reduce.2.cloned.1.call-update
  74.4 38.9 %psum.15 = f32[64]{0:T(128)S(1)} all-reduce(f32[64]{0:T(128)S(1)} %copy-done.6), channel_id=1, replica_groups=mesh['samp'=8,'sx'=2,'sy'=2] {'samp','sx','sy'}, use_global_device_ids=true, to_apply=%region_2.3 | all-reduce | flops 64 | bytes 512 | tf_op jit(solution)/shard_map/psum | solution.py:77
  113.4 0.5 broadcast_multiply_fusion.1
  113.9 0.0 collective-permute-done.5
  113.9 0.0 collective-permute-done.4
  113.9 0.2 pad_maximum_fusion.1
  114.1 0.3 fusion.45
  114.5 4.0 %collective-permute-start.7 = (bf16[1,64,4,1,128]{1,3,4,2,0:T(2,128)(2,1)S(1)}, bf16[1,64,4,1,128]{1,3,4,2,0:T(2,128)(2,1)S(1)}, u32[]{:S(2)}, u32[]{:S(2)}) collective-permute-start(bf16[1,64,4,1,128]{1,3,4,2,0:T(2,128)(2,1)S(1)} %get-tuple-element.23), channel_id=1, source_target_pairs={{1,0},{3,2},{5,4},{7,6},{9,8},{11,10},{13,12},{15,14},{17,16},{19,... | collective-permute-start | bytes 196616 | tf_op jit(solution)/shard_map/ppermute | solution.py:15
  118.5 1.3 collective-permute-start.6
  119.8 84.6 %all-reduce.2.cloned.1.call-done = f32[64,32,3,3,3]{0,1,4,3,2:T(8,128)} async-done(((f32[64,32,3,3,3]{0,1,4,3,2:T(8,128)}), f32[64,32,3,3,3]{0,1,4,3,2:T(8,128)}) %all-reduce.2.cloned.1.call-update) | async-done | bytes 221200 | tf_op jit(solution)/shard_map/psum | solution.py:77
  204.4 1.8 broadcast_multiply_fusion
  206.2 0.6 copy.60
  206.8 0.0 collective-permute-done.7
  206.8 0.1 copy.61
  207.0 0.0 collective-permute-done.6
  207.0 0.1 copy.59
  207.1 0.1 maximum_bitcast_fusion
  207.2 1.9 copy.70
  209.1 0.7 pad.2.clone
  209.8 0.0 copy-start.9
  209.8 0.2 copy.64
  210.0 0.4 copy-done.9
  210.4 4.0 %fusion.25 = bf16[2,8,8,17,32]{4,2,3,1,0:T(8,128)(2,1)S(1)} fusion(bf16[64,32,3,3,3]{0,1,4,3,2:T(8,128)(2,1)S(1)} %copy-done, bf16[64,4,10,1,7,2]{0,4,5,2,1,3:T(8,128)(2,1)S(1)} %slice.46, bf16[64,4,10,1,8,17]{0,4,5,2,1,3:T(8,128)(2,1)S(1)} %copy.64, pred[8,17]{0,1:T(8,128)(4,1)S(1)} %copy-done.9), kind=kOutput, calls=%fused_computation.21 | convolution fusion | flops 243122176 | bytes 1017992 | tf_op jit(solution)/shard_map/conv_general_dilated | solution.py:33
  214.5 0.1 copy.65
  214.6 1.0 copy.68
  (11 shorter events, 0.2 us)
Async XLA Ops:
  7.2 37.5 %copy-start = (bf16[64,32,3,3,3]{0,1,4,3,2:T(8,128)(2,1)S(1)}, bf16[64,32,3,3,3]{0,1,4,3,2:T(8,128)(2,1)}, u32[]{:S(2)}) copy-start(bf16[64,32,3,3,3]{0,1,4,3,2:T(8,128)(2,1)} %param.5) | copy-start | bytes 331780
  7.2 197.2 %all-reduce.2.cloned.1.call-start = ((), (), s32[]{:S(2)}) async-start(), calls=%async_computation | async-start | bytes 884736 | tf_op jit(solution)/shard_map/psum | solution.py:77
  8.2 7.1 %collective-permute-start.1 = (bf16[1,32,1,8,128]{4,3,2,1,0:T(8,128)(2,1)S(1)}, bf16[1,32,1,8,128]{4,3,2,1,0:T(8,128)(2,1)S(1)}, u32[]{:S(2)}, u32[]{:S(2)}) collective-permute-start(bf16[1,32,1,8,128]{4,3,2,1,0:T(8,128)(2,1)S(1)} %get-tuple-element.27), channel_id=1, source_target_pairs={{2,0},{3,1},{6,4},{7,5},{10,8},{11,9},{14,12},{15,13},{18,16},{19,... | collective-permute-start | bytes 196616 | tf_op jit(solution)/shard_map/ppermute | solution.py:15
  9.5 7.3 %collective-permute-start = (bf16[1,32,1,8,128]{4,3,2,1,0:T(8,128)(2,1)S(1)}, bf16[1,32,1,8,128]{4,3,2,1,0:T(8,128)(2,1)S(1)}, u32[]{:S(2)}, u32[]{:S(2)}) collective-permute-start(bf16[1,32,1,8,128]{4,3,2,1,0:T(8,128)(2,1)S(1)} %get-tuple-element.26), channel_id=1, source_target_pairs={{0,2},{1,3},{4,6},{5,7},{8,10},{9,11},{12,14},{13,15},{16,18},{17,... | collective-permute-start | bytes 196616 | tf_op jit(solution)/shard_map/ppermute | solution.py:14
  17.8 5.3 %copy-start.3 = (bf16[1,64,2,8,128]{4,3,2,1,0:T(8,128)(2,1)S(1)}, bf16[1,64,2,8,128]{4,3,2,1,0:T(8,128)(2,1)}, u32[]{:S(2)}) copy-start(bf16[1,64,2,8,128]{4,3,2,1,0:T(8,128)(2,1)} %param.7) | copy-start | bytes 786436
  20.3 6.9 %collective-permute-start.3 = (bf16[1,32,4,1,128]{1,0,4,3,2:T(2,128)(2,1)}, bf16[1,32,4,1,128]{1,0,4,3,2:T(2,128)(2,1)S(1)}, u32[]{:S(2)}, u32[]{:S(2)}) collective-permute-start(bf16[1,32,4,1,128]{1,0,4,3,2:T(2,128)(2,1)} %get-tuple-element.19), channel_id=1, source_target_pairs={{1,0},{3,2},{5,4},{7,6},{9,8},{11,10},{13,12},{15,14},{17,16},{19,... | collective-permute-start | bytes 98312 | tf_op jit(solution)/shard_map/ppermute | solution.py:15
  21.7 9.6 %collective-permute-start.2 = (bf16[1,32,4,1,128]{1,0,4,3,2:T(2,128)(2,1)}, bf16[1,32,4,1,128]{1,0,4,3,2:T(2,128)(2,1)}, u32[]{:S(2)}, u32[]{:S(2)}) collective-permute-start(bf16[1,32,4,1,128]{1,0,4,3,2:T(2,128)(2,1)} %get-tuple-element.18), channel_id=1, source_target_pairs={{0,1},{2,3},{4,5},{6,7},{8,9},{10,11},{12,13},{14,15},{16,17},{18,... | collective-permute-start | bytes 98312 | tf_op jit(solution)/shard_map/ppermute | solution.py:14
  44.4 0.7 copy-start.7
  44.4 0.7 copy-start.8
  48.8 1.7 copy-start.1
  50.5 15.8 %copy-start.2 = (bf16[2,8,8,17,64]{4,2,3,1,0:T(8,128)(2,1)S(1)}, bf16[2,8,8,17,64]{4,2,3,1,0:T(8,128)(2,1)}, u32[]{:S(2)}) copy-start(bf16[2,8,8,17,64]{4,2,3,1,0:T(8,128)(2,1)} %get-tuple-element.21) | copy-start | bytes 835588
  66.3 1.3 copy-start.5
  66.3 2.6 %copy-start.4 = (bf16[1,64,1,8,128]{1,3,4,2,0:T(8,128)(2,1)S(1)}, bf16[1,64,1,8,128]{1,3,4,2,0:T(8,128)(2,1)}, u32[]{:S(2)}) copy-start(bf16[1,64,1,8,128]{1,3,4,2,0:T(8,128)(2,1)} %get-tuple-element.24) | copy-start | bytes 393220
  66.4 8.0 %copy-start.6 = (f32[64]{0:T(128)S(1)}, f32[64]{0:T(128)}, u32[]{:S(2)}) copy-start(f32[64]{0:T(128)} %get-tuple-element.16) | copy-start | bytes 772
  67.6 46.3 %collective-permute-start.5 = (bf16[1,64,1,8,128]{1,3,4,2,0:T(8,128)(2,1)S(1)}, bf16[1,64,1,8,128]{1,3,4,2,0:T(8,128)(2,1)S(1)}, u32[]{:S(2)}, u32[]{:S(2)}) collective-permute-start(bf16[1,64,1,8,128]{1,3,4,2,0:T(8,128)(2,1)S(1)} %copy-done.5), channel_id=1, source_target_pairs={{2,0},{3,1},{6,4},{7,5},{10,8},{11,9},{14,12},{15,13},{18,16},{19,... | collective-permute-start | bytes 393224 | tf_op jit(solution)/shard_map/ppermute | solution.py:15
  68.9 45.0 %collective-permute-start.4 = (bf16[1,64,1,8,128]{1,3,4,2,0:T(8,128)(2,1)S(1)}, bf16[1,64,1,8,128]{1,3,4,2,0:T(8,128)(2,1)S(1)}, u32[]{:S(2)}, u32[]{:S(2)}) collective-permute-start(bf16[1,64,1,8,128]{1,3,4,2,0:T(8,128)(2,1)S(1)} %copy-done.4), channel_id=1, source_target_pairs={{0,2},{1,3},{4,6},{5,7},{8,10},{9,11},{12,14},{13,15},{16,18},{17,... | collective-permute-start | bytes 393224 | tf_op jit(solution)/shard_map/ppermute | solution.py:14
  114.5 92.3 %collective-permute-start.7 = (bf16[1,64,4,1,128]{1,3,4,2,0:T(2,128)(2,1)S(1)}, bf16[1,64,4,1,128]{1,3,4,2,0:T(2,128)(2,1)S(1)}, u32[]{:S(2)}, u32[]{:S(2)}) collective-permute-start(bf16[1,64,4,1,128]{1,3,4,2,0:T(2,128)(2,1)S(1)} %get-tuple-element.23), channel_id=1, source_target_pairs={{1,0},{3,2},{5,4},{7,6},{9,8},{11,10},{13,12},{15,14},{17,16},{19,... | collective-permute-start | bytes 196616 | tf_op jit(solution)/shard_map/ppermute | solution.py:15
  118.5 88.5 %collective-permute-start.6 = (bf16[1,64,4,1,128]{1,3,4,2,0:T(2,128)(2,1)S(1)}, bf16[1,64,4,1,128]{1,3,4,2,0:T(2,128)(2,1)S(1)}, u32[]{:S(2)}, u32[]{:S(2)}) collective-permute-start(bf16[1,64,4,1,128]{1,3,4,2,0:T(2,128)(2,1)S(1)} %get-tuple-element.22), channel_id=1, source_target_pairs={{0,1},{2,3},{4,5},{6,7},{8,9},{10,11},{12,13},{14,15},{16,17},{18,... | collective-permute-start | bytes 196616 | tf_op jit(solution)/shard_map/ppermute | solution.py:14
  209.8 0.7 copy-start.9
Sparse Core Ops, SparseCore 0:
  74.5 129.7 all-reduce.1
where the time goes:
time: 223 us; the launch traced here: 222 us
  waiting for transfers between devices  94.3 us (42%)
  blocking collectives  38.9 us (17%)
  matrix products  23.3 us (10%)
  starting transfers between devices  21.5 us (10%)
  local copies, waits for them, and re-layouts  18.9 us (8%)
  between operations  14.4 us (6%)
  other arithmetic  11.2 us (5%)
    psum x1, waiting for transfers between devices, per_device(): wsum, bsum = lax.psum((wgrad, bgrad), ('samp', 'sx', 'sy'))  84.6 us
    psum x1, blocking collectives, per_device(): wsum, bsum = lax.psum((wgrad, bgrad), ('samp', 'sx', 'sy'))  38.9 us
    conv_general_dilated x1, matrix products, filter_terms(): lax.conv_general_dilated(padded, delta, (1, 1, 1), ((0, 0), (0, 0), (1, 1...  15.8 us
    ppermute x4, starting transfers between devices, extended(): before = lax.ppermute(last, axis, up)  13.5 us
    concatenate x4, other arithmetic, extended(): shard = jnp.concatenate([before, shard, after], axis=dim)  8.04 us
    ppermute x4, starting transfers between devices, extended(): after = lax.ppermute(initial, axis, down)  7.99 us
    concatenate x5, local copies, waits for them, and re-layouts, extended(): shard = jnp.concatenate([before, shard, after], axis=dim)  7.9 us
    unnamed x25, local copies, waits for them, and re-layouts  6.4 us
  transfers between devices with their start and end apart: 9, of which 5 were waited for; matrix products, arithmetic and copies ran while one was open for 2% of the time, Pallas kernels for 0%

commit v1 on v0

--- a/solution.py
+++ b/solution.py
@@ -1,7 +1,17 @@
+import functools
 import jax
 import jax.numpy as jnp
 from jax import lax
 from jax.sharding import PartitionSpec as P
+
+
+def _finish_numbers(x_local, peer_axis, bus_axis):
+    for rr in (bus_axis, peer_axis):
+        x_local = lax.psum(x_local, rr)
+    return x_local
+
+
+sectors_feed = functools.partial(_finish_numbers, peer_axis="samp", bus_axis=("sx", "sy"))
 
 
 def extended(shard, sides, width):
@@ -74,7 +84,7 @@
     groups = lax.axis_size("sx") * lax.axis_size("sy")
     whole = lax.axis_size("samp") * samples * groups * rows * cols * depth
     norm = 1.0 / jnp.sqrt(jnp.float32(whole))
-    wsum, bsum = lax.psum((wgrad, bgrad), ("samp", "sx", "sy"))
+    wsum, bsum = sectors_feed((wgrad, bgrad))
     return (activated, input_grad, wsum * norm, bsum * norm)
 
 

time: 223 us -> 189 us (0.85)
  waiting for transfers between devices: 94.3 us -> 76.6 us
  blocking collectives: 38.9 us -> 23.6 us
  starting transfers between devices: 21.5 us -> 18.9 us
    psum x1 -> x2, waiting for transfers between devices: 84.6 us -> 54.8 us  [_finish_numbers(): x_local = lax.psum(x_local, rr)]
    psum x1 -> x2, blocking collectives: 38.9 us -> 23.6 us  [_finish_numbers(): x_local = lax.psum(x_local, rr)]
    ppermute x4, waiting for transfers between devices: 4.05 us -> 14.3 us  [extended(): after = lax.ppermute(initial, axis, down)]
    ppermute x4, starting transfers between devices: 7.99 us -> 5.3 us  [extended(): after = lax.ppermute(initial, axis, down)]
  transfers between devices with their start and end apart: 9 -> 10, of which waited for: 5 -> 7; matrix products, arithmetic and copies ran while one was open for 2% -> 6% of each run, Pallas kernels for 0% -> 0%
where the time goes in v1:
time: 189 us; the launch traced here: 187 us
  waiting for transfers between devices  76.6 us (41%)
  blocking collectives  23.6 us (12%)
  matrix products  23.3 us (12%)
  local copies, waits for them, and re-layouts  18.9 us (10%)
  starting transfers between devices  18.9 us (10%)
  between operations  14.4 us (8%)
  other arithmetic  11.1 us (6%)
    psum x2, waiting for transfers between devices, _finish_numbers(): x_local = lax.psum(x_local, rr)  54.8 us
    psum x2, blocking collectives, _finish_numbers(): x_local = lax.psum(x_local, rr)  23.6 us
    conv_general_dilated x1, matrix products, filter_terms(): lax.conv_general_dilated(padded, delta, (1, 1, 1), ((0, 0), (0, 0), (1, 1...  15.8 us
    ppermute x4, waiting for transfers between devices, extended(): after = lax.ppermute(initial, axis, down)  14.3 us
    ppermute x4, starting transfers between devices, extended(): before = lax.ppermute(last, axis, up)  13.5 us
    concatenate x4, other arithmetic, extended(): shard = jnp.concatenate([before, shard, after], axis=dim)  8.01 us
    concatenate x5, local copies, waits for them, and re-layouts, extended(): shard = jnp.concatenate([before, shard, after], axis=dim)  7.9 us
    ppermute x4, waiting for transfers between devices, extended(): before = lax.ppermute(last, axis, up)  7.45 us
  transfers between devices with their start and end apart: 10, of which 7 were waited for; matrix products, arithmetic and copies ran while one was open for 6% of the time, Pallas kernels for 0%

profile of v1, /device:TPU:8, one launch (start us, length us, event | category | flops | bytes accessed | tf_op | source)
XLA Modules:
  0.0 186.7 jit_solution(8286435160365967825)
XLA Ops:
  7.2 0.0 copy-start
  7.2 0.0 all-reduce.3.cloned.1.call-start
  7.2 0.9 fusion.47
  8.2 1.3 collective-permute-start.1
  9.5 5.4 %collective-permute-start = (bf16[1,32,1,8,128]{4,3,2,1,0:T(8,128)(2,1)S(1)}, bf16[1,32,1,8,128]{4,3,2,1,0:T(8,128)(2,1)S(1)}, u32[]{:S(2)}, u32[]{:S(2)}) collective-permute-start(bf16[1,32,1,8,128]{4,3,2,1,0:T(8,128)(2,1)S(1)} %get-tuple-element.26), channel_id=1, source_target_pairs={{0,2},{1,3},{4,6},{5,7},{8,10},{9,11},{12,14},{13,15},{16,18},{17,... | collective-permute-start | bytes 196616 | tf_op jit(solution)/shard_map/ppermute | solution.py:24
  14.9 0.3 collective-permute-done.1
  15.2 1.6 collective-permute-done
  16.8 1.0 pad_maximum_fusion.2
  17.8 0.0 copy-start.3
  17.8 1.2 copy.49
  19.0 1.3 fusion.44
  20.3 1.4 collective-permute-start.3
  21.7 1.3 collective-permute-start.2
  23.0 0.4 copy.57
  23.4 3.7 %collective-permute-done.3 = bf16[1,32,4,1,128]{1,0,4,3,2:T(2,128)(2,1)S(1)} collective-permute-done((bf16[1,32,4,1,128]{1,0,4,3,2:T(2,128)(2,1)}, bf16[1,32,4,1,128]{1,0,4,3,2:T(2,128)(2,1)S(1)}, u32[]{:S(2)}, u32[]{:S(2)}) %collective-permute-start.3) | collective-permute-done | bytes 32800 | tf_op jit(solution)/shard_map/ppermute | solution.py:25
  27.2 4.1 %collective-permute-done.2 = bf16[1,32,4,1,128]{1,0,4,3,2:T(2,128)(2,1)} collective-permute-done((bf16[1,32,4,1,128]{1,0,4,3,2:T(2,128)(2,1)}, bf16[1,32,4,1,128]{1,0,4,3,2:T(2,128)(2,1)}, u32[]{:S(2)}, u32[]{:S(2)}) %collective-permute-start.2) | collective-permute-done | bytes 32800 | tf_op jit(solution)/shard_map/ppermute | solution.py:24
  31.3 6.7 %pad_maximum_fusion = bf16[1,32,4,10,128]{1,0,4,3,2:T(2,128)(2,1)} fusion(bf16[1,32,4,1,128]{1,0,4,3,2:T(2,128)(2,1)S(1)} %collective-permute-done.3, bf16[1,32,4,8,128]{1,0,4,3,2:T(2,128)(2,1)S(1)} %copy.49, bf16[1,32,4,1,128]{1,0,4,3,2:T(2,128)(2,1)} %collective-permute-done.2), kind=kLoop, calls=%fused_computation.5 | loop fusion | flops 327680 | bytes 655360 | tf_op jit(solution)/shard_map/concatenate | solution.py:26
  38.0 4.7 %copy.52 = bf16[1,32,4,10,128]{4,1,3,2,0:T(8,128)(2,1)S(1)} copy(bf16[1,32,4,10,128]{1,0,4,3,2:T(2,128)(2,1)} %pad_maximum_fusion) | data formatting | bytes 655360 | tf_op jit(solution)/shard_map/concatenate | solution.py:26
  42.7 1.0 copy.69
  43.7 0.7 pad.clone
  44.4 0.0 copy-start.7
  44.4 0.0 copy-start.8
  44.4 0.2 copy.55
  44.7 0.4 copy-done.7
  45.1 0.0 copy-done.8
  45.1 3.4 %multiply_add_fusion = (f32[2,8,8,17,64]{4,2,3,1,0:T(8,128)S(1)}, bf16[2,8,8,17,64]{4,2,3,1,0:T(8,128)(2,1)}) fusion(f32[64]{0:T(128)S(1)} %copy-done.7, bf16[64,32,3,3,3]{0,1,4,3,2:T(8,128)(2,1)S(1)} %copy-done, bf16[32,4,10,1,7,2]{0,4,5,2,1,3:T(8,128)(2,1)S(1)} %slice.39, bf16[32,4,10,1,8,17]{0,4,5,2,1,3:T(8,128)(2,1)S(1)} %copy.55, ...), kind=kOutput, calls=%fused_computation.25 | convolution fusion | flops 244183040 | bytes 1330568 | tf_op jit(solution)/shard_map/conv_general_dilated | solution.py:31
  48.5 0.2 copy.58
  48.8 0.8 convert_reduce_fusion
  49.6 0.8 fusion.46
  50.4 0.1 copy-done.1
  50.5 15.8 %fusion.33 = f32[64,32,3,3,3]{0,1,4,3,2:T(8,128)} fusion(bf16[1,32,4,10,128]{1,0,4,3,2:T(2,128)(2,1)S(1)} %copy-done.1, bf16[1,64,2,8,128]{1,3,4,2,0:T(8,128)(2,1)S(1)} %get-tuple-element.17), kind=kOutput, calls=%fused_computation.31 | convolution fusion | flops 225312768 | bytes 811008 | tf_op jit(solution)/shard_map/conv_general_dilated | solution.py:54
  66.3 0.1 copy.56
  66.4 0.0 copy-start.6
  66.4 1.3 collective-permute-start.5
  67.7 5.5 %collective-permute-start.4 = (bf16[1,64,1,8,128]{1,3,4,2,0:T(8,128)(2,1)S(1)}, bf16[1,64,1,8,128]{1,3,4,2,0:T(8,128)(2,1)S(1)}, u32[]{:S(2)}, u32[]{:S(2)}) collective-permute-start(bf16[1,64,1,8,128]{1,3,4,2,0:T(8,128)(2,1)S(1)} %copy-done.4), channel_id=1, source_target_pairs={{0,2},{1,3},{4,6},{5,7},{8,10},{9,11},{12,14},{13,15},{16,18},{17,... | collective-permute-start | bytes 393224 | tf_op jit(solution)/shard_map/ppermute | solution.py:24
  73.2 1.1 copy.67
  74.4 0.0 all-reduce.3.cloned.1.call-update
  74.4 0.0 all-reduce.5.cloned.1.call-start
  74.5 11.8 %psum.30 = f32[64]{0:T(128)S(1)} all-reduce(f32[64]{0:T(128)S(1)} %copy-done.6), channel_id=1, replica_groups=mesh['samp'=8,'sx'=2,'sy'=2] {'sx','sy'}, use_global_device_ids=true, to_apply=%region_3.4 | all-reduce | flops 64 | bytes 512 | tf_op jit(solution)/shard_map/psum | solution.py:10
  86.2 11.8 %psum.31 = f32[64]{0:T(128)S(1)} all-reduce(f32[64]{0:T(128)S(1)} %psum.30), channel_id=1, replica_groups=mesh['samp'=8,'sx'=2,'sy'=2] {'samp'}, use_global_device_ids=true, to_apply=%region_4.5 | all-reduce | flops 64 | bytes 512 | tf_op jit(solution)/shard_map/psum | solution.py:10
  98.0 0.0 collective-permute-done.5
  98.0 0.2 pad_maximum_fusion.1
  98.3 0.3 fusion.45
  98.6 1.3 collective-permute-start.7
  100.0 1.3 collective-permute-start.6
  101.3 0.5 broadcast_multiply_fusion.1
  101.8 0.6 copy.60
  102.4 10.2 %collective-permute-done.7 = bf16[1,64,4,1,128]{1,3,4,2,0:T(2,128)(2,1)S(1)} collective-permute-done((bf16[1,64,4,1,128]{1,3,4,2,0:T(2,128)(2,1)S(1)}, bf16[1,64,4,1,128]{1,3,4,2,0:T(2,128)(2,1)S(1)}, u32[]{:S(2)}, u32[]{:S(2)}) %collective-permute-start.7) | collective-permute-done | bytes 65568 | tf_op jit(solution)/shard_map/ppermute | solution.py:25
  112.6 0.1 copy.61
  112.8 1.7 collective-permute-done.6
  114.5 0.1 copy.59
  114.6 0.1 maximum_bitcast_fusion
  114.7 1.9 copy.70
  116.6 0.7 pad.2.clone
  117.3 0.0 copy-start.9
  117.3 0.2 copy.64
  117.5 0.4 copy-done.9
  118.0 4.0 %fusion.25 = bf16[2,8,8,17,32]{4,2,3,1,0:T(8,128)(2,1)S(1)} fusion(bf16[64,32,3,3,3]{0,1,4,3,2:T(8,128)(2,1)S(1)} %copy-done, bf16[64,4,10,1,7,2]{0,4,5,2,1,3:T(8,128)(2,1)S(1)} %slice.46, bf16[64,4,10,1,8,17]{0,4,5,2,1,3:T(8,128)(2,1)S(1)} %copy.64, pred[8,17]{0,1:T(8,128)(4,1)S(1)} %copy-done.9), kind=kOutput, calls=%fused_computation.21 | convolution fusion | flops 243122176 | bytes 1017992 | tf_op jit(solution)/shard_map/conv_general_dilated | solution.py:43
  122.0 0.1 copy.65
  122.1 0.0 all-reduce.3.cloned.1.call-done
  122.1 0.0 all-reduce.5.cloned.1.call-update
  122.2 1.0 copy.68
  123.2 54.8 %all-reduce.5.cloned.1.call-done = f32[64,32,3,3,3]{0,1,4,3,2:T(8,128)} async-done(((f32[64,32,3,3,3]{0,1,4,3,2:T(8,128)}), f32[64,32,3,3,3]{0,1,4,3,2:T(8,128)}) %all-reduce.5.cloned.1.call-update) | async-done | bytes 221200 | tf_op jit(solution)/shard_map/psum | solution.py:10
  178.0 1.8 broadcast_multiply_fusion
  (15 shorter events, 0.2 us)
Async XLA Ops:
  7.2 37.5 %copy-start = (bf16[64,32,3,3,3]{0,1,4,3,2:T(8,128)(2,1)S(1)}, bf16[64,32,3,3,3]{0,1,4,3,2:T(8,128)(2,1)}, u32[]{:S(2)}) copy-start(bf16[64,32,3,3,3]{0,1,4,3,2:T(8,128)(2,1)} %param.5) | copy-start | bytes 331780
  7.2 114.9 %all-reduce.3.cloned.1.call-start = ((), (), s32[]{:S(2)}) async-start(), calls=%async_computation | async-start | bytes 884736 | tf_op jit(solution)/shard_map/psum | solution.py:10
  8.2 7.1 %collective-permute-start.1 = (bf16[1,32,1,8,128]{4,3,2,1,0:T(8,128)(2,1)S(1)}, bf16[1,32,1,8,128]{4,3,2,1,0:T(8,128)(2,1)S(1)}, u32[]{:S(2)}, u32[]{:S(2)}) collective-permute-start(bf16[1,32,1,8,128]{4,3,2,1,0:T(8,128)(2,1)S(1)} %get-tuple-element.27), channel_id=1, source_target_pairs={{2,0},{3,1},{6,4},{7,5},{10,8},{11,9},{14,12},{15,13},{18,16},{19,... | collective-permute-start | bytes 196616 | tf_op jit(solution)/shard_map/ppermute | solution.py:25
  9.5 7.3 %collective-permute-start = (bf16[1,32,1,8,128]{4,3,2,1,0:T(8,128)(2,1)S(1)}, bf16[1,32,1,8,128]{4,3,2,1,0:T(8,128)(2,1)S(1)}, u32[]{:S(2)}, u32[]{:S(2)}) collective-permute-start(bf16[1,32,1,8,128]{4,3,2,1,0:T(8,128)(2,1)S(1)} %get-tuple-element.26), channel_id=1, source_target_pairs={{0,2},{1,3},{4,6},{5,7},{8,10},{9,11},{12,14},{13,15},{16,18},{17,... | collective-permute-start | bytes 196616 | tf_op jit(solution)/shard_map/ppermute | solution.py:24
  17.8 5.3 %copy-start.3 = (bf16[1,64,2,8,128]{4,3,2,1,0:T(8,128)(2,1)S(1)}, bf16[1,64,2,8,128]{4,3,2,1,0:T(8,128)(2,1)}, u32[]{:S(2)}) copy-start(bf16[1,64,2,8,128]{4,3,2,1,0:T(8,128)(2,1)} %param.7) | copy-start | bytes 786436
  20.3 6.9 %collective-permute-start.3 = (bf16[1,32,4,1,128]{1,0,4,3,2:T(2,128)(2,1)}, bf16[1,32,4,1,128]{1,0,4,3,2:T(2,128)(2,1)S(1)}, u32[]{:S(2)}, u32[]{:S(2)}) collective-permute-start(bf16[1,32,4,1,128]{1,0,4,3,2:T(2,128)(2,1)} %get-tuple-element.19), channel_id=1, source_target_pairs={{1,0},{3,2},{5,4},{7,6},{9,8},{11,10},{13,12},{15,14},{17,16},{19,... | collective-permute-start | bytes 98312 | tf_op jit(solution)/shard_map/ppermute | solution.py:25
  21.7 9.6 %collective-permute-start.2 = (bf16[1,32,4,1,128]{1,0,4,3,2:T(2,128)(2,1)}, bf16[1,32,4,1,128]{1,0,4,3,2:T(2,128)(2,1)}, u32[]{:S(2)}, u32[]{:S(2)}) collective-permute-start(bf16[1,32,4,1,128]{1,0,4,3,2:T(2,128)(2,1)} %get-tuple-element.18), channel_id=1, source_target_pairs={{0,1},{2,3},{4,5},{6,7},{8,9},{10,11},{12,13},{14,15},{16,17},{18,... | collective-permute-start | bytes 98312 | tf_op jit(solution)/shard_map/ppermute | solution.py:24
  44.4 0.7 copy-start.7
  44.4 0.7 copy-start.8
  48.7 1.7 copy-start.1
  50.5 15.8 %copy-start.2 = (bf16[2,8,8,17,64]{4,2,3,1,0:T(8,128)(2,1)S(1)}, bf16[2,8,8,17,64]{4,2,3,1,0:T(8,128)(2,1)}, u32[]{:S(2)}) copy-start(bf16[2,8,8,17,64]{4,2,3,1,0:T(8,128)(2,1)} %get-tuple-element.21) | copy-start | bytes 835588
  50.5 15.9 %copy-start.5 = (bf16[1,64,1,8,128]{1,3,4,2,0:T(8,128)(2,1)S(1)}, bf16[1,64,1,8,128]{1,3,4,2,0:T(8,128)(2,1)}, u32[]{:S(2)}) copy-start(bf16[1,64,1,8,128]{1,3,4,2,0:T(8,128)(2,1)} %get-tuple-element.25) | copy-start | bytes 393220
  50.5 17.2 %copy-start.4 = (bf16[1,64,1,8,128]{1,3,4,2,0:T(8,128)(2,1)S(1)}, bf16[1,64,1,8,128]{1,3,4,2,0:T(8,128)(2,1)}, u32[]{:S(2)}) copy-start(bf16[1,64,1,8,128]{1,3,4,2,0:T(8,128)(2,1)} %get-tuple-element.24) | copy-start | bytes 393220
  66.4 8.1 %copy-start.6 = (f32[64]{0:T(128)S(1)}, f32[64]{0:T(128)}, u32[]{:S(2)}) copy-start(f32[64]{0:T(128)} %get-tuple-element.16) | copy-start | bytes 772
  66.4 31.6 %collective-permute-start.5 = (bf16[1,64,1,8,128]{1,3,4,2,0:T(8,128)(2,1)S(1)}, bf16[1,64,1,8,128]{1,3,4,2,0:T(8,128)(2,1)S(1)}, u32[]{:S(2)}, u32[]{:S(2)}) collective-permute-start(bf16[1,64,1,8,128]{1,3,4,2,0:T(8,128)(2,1)S(1)} %copy-done.5), channel_id=1, source_target_pairs={{2,0},{3,1},{6,4},{7,5},{10,8},{11,9},{14,12},{15,13},{18,16},{19,... | collective-permute-start | bytes 393224 | tf_op jit(solution)/shard_map/ppermute | solution.py:25
  67.7 30.3 %collective-permute-start.4 = (bf16[1,64,1,8,128]{1,3,4,2,0:T(8,128)(2,1)S(1)}, bf16[1,64,1,8,128]{1,3,4,2,0:T(8,128)(2,1)S(1)}, u32[]{:S(2)}, u32[]{:S(2)}) collective-permute-start(bf16[1,64,1,8,128]{1,3,4,2,0:T(8,128)(2,1)S(1)} %copy-done.4), channel_id=1, source_target_pairs={{0,2},{1,3},{4,6},{5,7},{8,10},{9,11},{12,14},{13,15},{16,18},{17,... | collective-permute-start | bytes 393224 | tf_op jit(solution)/shard_map/ppermute | solution.py:24
  74.4 103.6 %all-reduce.5.cloned.1.call-start = ((), (), s32[]{:S(2)}) async-start(), calls=%async_computation.1 | async-start | bytes 884736 | tf_op jit(solution)/shard_map/psum | solution.py:10
  98.6 14.0 %collective-permute-start.7 = (bf16[1,64,4,1,128]{1,3,4,2,0:T(2,128)(2,1)S(1)}, bf16[1,64,4,1,128]{1,3,4,2,0:T(2,128)(2,1)S(1)}, u32[]{:S(2)}, u32[]{:S(2)}) collective-permute-start(bf16[1,64,4,1,128]{1,3,4,2,0:T(2,128)(2,1)S(1)} %get-tuple-element.23), channel_id=1, source_target_pairs={{1,0},{3,2},{5,4},{7,6},{9,8},{11,10},{13,12},{15,14},{17,16},{19,... | collective-permute-start | bytes 196616 | tf_op jit(solution)/shard_map/ppermute | solution.py:25
  100.0 14.5 %collective-permute-start.6 = (bf16[1,64,4,1,128]{1,3,4,2,0:T(2,128)(2,1)S(1)}, bf16[1,64,4,1,128]{1,3,4,2,0:T(2,128)(2,1)S(1)}, u32[]{:S(2)}, u32[]{:S(2)}) collective-permute-start(bf16[1,64,4,1,128]{1,3,4,2,0:T(2,128)(2,1)S(1)} %get-tuple-element.22), channel_id=1, source_target_pairs={{0,1},{2,3},{4,5},{6,7},{8,9},{10,11},{12,13},{14,15},{16,17},{18,... | collective-permute-start | bytes 196616 | tf_op jit(solution)/shard_map/ppermute | solution.py:24
  117.3 0.7 copy-start.9
Sparse Core Ops, SparseCore 0:
  74.5 39.9 all-reduce.2
  122.3 55.6 all-reduce.4
